TPU v7x, 32 devices: a whole 2x2x4 slice. The times are simulated.
32 devices in a mesh: fsdp: 8 (over z, y), tp: 4 (over x, core).
Axes of the slice: x: 2, y: 2, z: 4, core: 2. Of those that a mesh axis runs over, the one named last changes fastest.
Arguments:
- inputs: bfloat16 [4096, 1024], P(('fsdp', 'tp')), may hold values from -6 to 6
- cotangent: bfloat16 [4096, 1024], P(('fsdp', 'tp')), may hold values from -6 to 6
- lengths: int32 [8, 8], P('fsdp'), may hold values from 1 to 256, 512 in all within a row
- qkv_weight: bfloat16 [2, 3, 1024, 1024], P(None, None, 'fsdp', 'tp'), as said below
- qv_bias: bfloat16 [2, 2, 1024], P(None, None, ('tp', 'fsdp')), may hold values from -3 to 3
- out_weight: bfloat16 [2, 1024, 1024], P(None, 'tp', 'fsdp'), may hold values from -1 to 1
- fc_weight: bfloat16 [2, 1024, 4096], P(None, 'fsdp', 'tp'), may hold values from -0.1875 to 0.1875
- fc_bias: bfloat16 [2, 4096], P(None, ('tp', 'fsdp')), may hold values from -3 to 3
- proj_weight: bfloat16 [2, 4096, 1024], P(None, 'tp', 'fsdp'), may hold values from -0.09375 to 0.09375
- norm_gains: float32 [2, 2, 1024], P(None, None, ('fsdp', 'tp')), may hold values from 0.25 to 1.75
- shifts: float32 [2, 4, 1024], P(None, None, ('fsdp', 'tp')), may hold values from -3 to 3
Outputs:
- out_acts: bfloat16 [4096, 1024], P(('fsdp', 'tp'))
- in_grad: float32 [4096, 1024], P(('fsdp', 'tp'))
- qkv_grad: float32 [2, 3, 1024, 1024], P(None, None, 'fsdp', 'tp')
- qv_bias_grad: float32 [2, 2, 1024], P(None, None, ('tp', 'fsdp'))
- out_grad: float32 [2, 1024, 1024], P(None, 'tp', 'fsdp')
- fc_grad: float32 [2, 1024, 4096], P(None, 'fsdp', 'tp')
- fc_bias_grad: float32 [2, 4096], P(None, ('tp', 'fsdp'))
- proj_grad: float32 [2, 4096, 1024], P(None, 'tp', 'fsdp')
- gains_grad: float32 [2, 2, 1024], P(None, None, ('fsdp', 'tp'))
- shifts_grad: float32 [2, 4, 1024], P(None, None, ('fsdp', 'tp'))
Inputs may be any that keep to these rules, and one draw needn't show every extreme that they name: Row g holds the lengths of group g's sequences in row order; they sum to 512 and the longest is 256. `qkv_weight`: columns h * 64 to (h + 1) * 64 - 1 of each projection belong to head h. Every entry lies between -6 / sqrt(1024) and 6 / sqrt(1024).
All inputs are finite; a program needn't handle non-finite values.
Results may differ from a plain program's by a relative error of at most 0.023.
Values may be sent and summed in bfloat16 or wider, within the bound.
No kernel may reach another device: no remote copies, remote signals or barrier semaphores. Data moves between devices by JAX's collectives and lax.ppermute only.
A program may use at most 128 MiB of HBM per device.

v0:
```python
import jax
import jax.numpy as jnp
from jax import lax
from jax.sharding import PartitionSpec as P

HEAD_DIM = 64
LAYERS = 2
eps_norm = 1e-05


def norm_stats(values):
    centre = values - jnp.mean(values, axis=-1, keepdims=True)
    variance = jnp.mean(centre * centre, axis=-1, keepdims=True)
    inv_std = lax.rsqrt(variance + eps_norm)
    return (centre * inv_std, inv_std)


def norm_back(d_normed, normed, inv_std):
    return inv_std * (
        d_normed
        - jnp.mean(d_normed, axis=-1, keepdims=True)
        - normed * jnp.mean(d_normed * normed, axis=-1, keepdims=True)
    )


def gelu_tanh(values):
    return jax.nn.gelu(values, approximate=True)


def gelu_back(pre_act, d_act):
    return jax.vjp(gelu_tanh, pre_act)[1](d_act)[0]


def allowed_pairs(seq_lens, group_len):
    bounds = jnp.cumsum(seq_lens)
    positions = jnp.arange(group_len, dtype=jnp.int32)
    segment = jnp.sum((positions[:, None] >= bounds[None, :]).astype(jnp.int32), axis=1)
    return (segment[:, None] == segment[None, :]) & (positions[None, :] <= positions[:, None])


def head_split(values):
    return values.reshape(values.shape[0], -1, HEAD_DIM)


def scores_of(queries, keys_in, allowed):
    raw = jnp.einsum(
        "qhd,khd->hqk", head_split(queries), head_split(keys_in), preferred_element_type=jnp.float32
    ) * HEAD_DIM ** (-0.5)
    return jnp.where(allowed[None], raw, -1e30)


def attend(queries, keys_in, values_in, allowed):
    scores = scores_of(queries, keys_in, allowed)
    row_top = jnp.max(scores, axis=-1)
    log_total = row_top + jnp.log(jnp.sum(jnp.exp(scores - row_top[..., None]), axis=-1))
    prob_low = jnp.exp(scores - log_total[..., None]).astype(jnp.bfloat16)
    mixed_heads = jnp.einsum(
        "hqk,khd->qhd", prob_low, head_split(values_in), preferred_element_type=jnp.float32
    )
    return (mixed_heads.reshape(mixed_heads.shape[0], -1).astype(jnp.bfloat16), log_total)


def attend_back(queries, keys_in, values_in, mixed_heads, log_total, d_mixed, allowed):
    scores = scores_of(queries, keys_in, allowed)
    probs = jnp.exp(scores - log_total[..., None])
    prob_low = probs.astype(jnp.bfloat16)
    dm_heads = head_split(d_mixed)
    d_values = jnp.einsum("hqk,qhd->khd", prob_low, dm_heads, preferred_element_type=jnp.float32)
    d_probs = jnp.einsum(
        "qhd,khd->hqk", dm_heads, head_split(values_in), preferred_element_type=jnp.float32
    )
    row_dot = jnp.transpose(
        jnp.sum(head_split(mixed_heads).astype(jnp.float32) * dm_heads.astype(jnp.float32), axis=-1)
    )
    d_scores = (probs * (d_probs - row_dot[:, :, None])).astype(jnp.bfloat16)
    scale = HEAD_DIM ** (-0.5)
    d_queries = (
        jnp.einsum(
            "hqk,khd->qhd", d_scores, head_split(keys_in), preferred_element_type=jnp.float32
        )
        * scale
    )
    d_keys = (
        jnp.einsum(
            "hqk,qhd->khd", d_scores, head_split(queries), preferred_element_type=jnp.float32
        )
        * scale
    )
    group_len = queries.shape[0]
    return (
        d_queries.reshape(group_len, -1),
        d_keys.reshape(group_len, -1),
        d_values.reshape(group_len, -1),
    )


def gather_acts(values):
    return lax.all_gather(values, "tp", axis=0, tiled=True)


def gather_grads(values):
    return lax.all_gather(values, "tp", axis=0, tiled=True)


def sum_branch(partial_fn, tok_rows):
    return lax.psum_scatter(
        partial_fn(jnp.int32(0), tok_rows * lax.axis_size("tp")),
        "tp",
        scatter_dimension=0,
        tiled=True,
    )


def sum_inputs(partial_fn, tok_rows):
    return lax.psum_scatter(
        partial_fn(jnp.int32(0), tok_rows * lax.axis_size("tp")).astype(jnp.bfloat16),
        "tp",
        scatter_dimension=0,
        tiled=True,
    ).astype(jnp.float32)


def contract_first(left, right):
    return lax.dot_general(
        left, right, (((0,), (0,)), ((), ())), preferred_element_type=jnp.float32
    )


def contract_last(left, right):
    return lax.dot_general(
        left, right, (((1,), (1,)), ((), ())), preferred_element_type=jnp.float32
    )


def body(
    inputs,
    cotangent,
    lengths,
    qkv_weight,
    qv_bias,
    out_weight,
    fc_weight,
    fc_bias,
    proj_weight,
    norm_gains,
    shifts,
):
    tok_rows = inputs.shape[0]
    group_len = tok_rows * lax.axis_size("tp")
    gains_all, shifts_all = (
        lax.all_gather(norm_gains, ("fsdp", "tp"), axis=2, tiled=True),
        lax.all_gather(shifts, ("fsdp", "tp"), axis=2, tiled=True),
    )
    allowed = allowed_pairs(lengths[0], group_len)
    residual = inputs.astype(jnp.float32)
    saved_acts = []
    for layer_id in range(LAYERS):
        weights = (
            lax.all_gather(qkv_weight[layer_id], "fsdp", axis=1, tiled=True),
            lax.all_gather(out_weight[layer_id], "fsdp", axis=1, tiled=True),
            lax.all_gather(fc_weight[layer_id], "fsdp", axis=0, tiled=True),
            lax.all_gather(proj_weight[layer_id], "fsdp", axis=1, tiled=True),
            lax.all_gather(qv_bias[layer_id], "fsdp", axis=1, tiled=True),
            lax.all_gather(fc_bias[layer_id], "fsdp", axis=0, tiled=True),
        )
        w_qkv, w_out, w_fc, w_proj, b_qv, b_fc = weights
        norm_gain = gains_all[layer_id]
        offset_rows = shifts_all[layer_id]
        normed_one, inv_one = norm_stats(residual)
        act_one = gather_acts((normed_one * norm_gain[0] + offset_rows[0]).astype(jnp.bfloat16))
        bias_rows = jnp.stack(
            [
                b_qv[0].astype(jnp.float32),
                jnp.zeros(b_qv[0].shape, jnp.float32),
                b_qv[1].astype(jnp.float32),
            ]
        )
        projected = (
            jnp.einsum("gd,cdh->cgh", act_one, w_qkv, preferred_element_type=jnp.float32)
            + bias_rows[:, None, :]
        )
        projected = projected.astype(jnp.bfloat16)
        mixed_heads, log_total = attend(projected[0], projected[1], projected[2], allowed)

        def out_part(first_row, row_count, mixed_heads=mixed_heads, w_out=w_out):
            return jnp.dot(mixed_heads, w_out, preferred_element_type=jnp.float32)

        middle = residual + sum_branch(out_part, tok_rows) + offset_rows[2]
        normed_two, inv_two = norm_stats(middle)
        act_two = gather_acts((normed_two * norm_gain[1] + offset_rows[1]).astype(jnp.bfloat16))
        pre_act = jnp.dot(act_two, w_fc, preferred_element_type=jnp.float32) + b_fc.astype(
            jnp.float32
        )
        hidden = gelu_tanh(pre_act).astype(jnp.bfloat16)

        def mlp_part(first_row, row_count, hidden=hidden, w_proj=w_proj):
            return jnp.dot(hidden, w_proj, preferred_element_type=jnp.float32)

        after_block = middle + sum_branch(mlp_part, tok_rows) + offset_rows[3]
        saved_acts.append(
            (residual, act_one, projected, mixed_heads, log_total, middle, act_two, pre_act, hidden)
        )
        residual = after_block
    out_rows = residual.astype(jnp.bfloat16)
    d_res = cotangent.astype(jnp.float32)
    gain_list = [None] * LAYERS
    shift_list = [None] * LAYERS
    grad_list = [None] * LAYERS
    for layer_id in reversed(range(LAYERS)):
        weights = (
            lax.all_gather(qkv_weight[layer_id], "fsdp", axis=1, tiled=True),
            lax.all_gather(out_weight[layer_id], "fsdp", axis=1, tiled=True),
            lax.all_gather(fc_weight[layer_id], "fsdp", axis=0, tiled=True),
            lax.all_gather(proj_weight[layer_id], "fsdp", axis=1, tiled=True),
            lax.all_gather(qv_bias[layer_id], "fsdp", axis=1, tiled=True),
            lax.all_gather(fc_bias[layer_id], "fsdp", axis=0, tiled=True),
        )
        w_qkv, w_out, w_fc, w_proj, b_qv, b_fc = weights
        norm_gain = gains_all[layer_id]
        residual, act_one, projected, mixed_heads, log_total, middle, act_two, pre_act, hidden = (
            saved_acts[layer_id]
        )
        d_after = d_res
        d_low = gather_grads(d_after.astype(jnp.bfloat16))
        d_proj = contract_first(hidden, d_low)
        d_hidden = contract_last(d_low, w_proj)
        d_pre = gelu_back(pre_act, d_hidden)
        d_pre_low = d_pre.astype(jnp.bfloat16)
        d_fc = contract_first(act_two, d_pre_low)
        d_fc_bias = jnp.sum(d_pre, axis=0)

        def fc_part(first_row, row_count, d_pre_low=d_pre_low, w_fc=w_fc):
            return contract_last(d_pre_low, w_fc)

        d_act_two = sum_inputs(fc_part, tok_rows)
        normed_two, inv_two = norm_stats(middle)
        d_middle = d_after + norm_back(d_act_two * norm_gain[1], normed_two, inv_two)
        d_mid_low = gather_grads(d_middle.astype(jnp.bfloat16))
        d_out = contract_first(mixed_heads, d_mid_low)
        d_mixed = contract_last(d_mid_low, w_out).astype(jnp.bfloat16)
        d_queries, d_keys, d_values = attend_back(
            projected[0], projected[1], projected[2], mixed_heads, log_total, d_mixed, allowed
        )
        d_bias = jnp.stack([jnp.sum(d_queries, axis=0), jnp.sum(d_values, axis=0)])
        d_proj_low = jnp.stack([d_queries, d_keys, d_values]).astype(jnp.bfloat16)
        d_qkv = jnp.einsum("gd,cgh->cdh", act_one, d_proj_low, preferred_element_type=jnp.float32)

        def qkv_part(first_row, row_count, d_proj_low=d_proj_low, w_qkv=w_qkv):
            return jnp.einsum("cgh,cdh->gd", d_proj_low, w_qkv, preferred_element_type=jnp.float32)

        d_act_one = sum_inputs(qkv_part, tok_rows)
        normed_one, inv_one = norm_stats(residual)
        d_res = d_middle + norm_back(d_act_one * norm_gain[0], normed_one, inv_one)
        gain_list[layer_id] = jnp.stack(
            [jnp.sum(d_act_one * normed_one, axis=0), jnp.sum(d_act_two * normed_two, axis=0)]
        )
        shift_list[layer_id] = jnp.stack(
            [
                jnp.sum(d_act_one, axis=0),
                jnp.sum(d_act_two, axis=0),
                jnp.sum(d_middle, axis=0),
                jnp.sum(d_after, axis=0),
            ]
        )
        layer_grads = (d_qkv, d_bias, d_out, d_fc, d_fc_bias, d_proj)
        grad_list[layer_id] = (
            lax.psum_scatter(
                layer_grads[0].astype(jnp.bfloat16), "fsdp", scatter_dimension=1, tiled=True
            ).astype(jnp.float32),
            lax.psum_scatter(
                layer_grads[1].astype(jnp.bfloat16), "fsdp", scatter_dimension=1, tiled=True
            ).astype(jnp.float32),
            lax.psum_scatter(
                layer_grads[2].astype(jnp.bfloat16), "fsdp", scatter_dimension=1, tiled=True
            ).astype(jnp.float32),
            lax.psum_scatter(
                layer_grads[3].astype(jnp.bfloat16), "fsdp", scatter_dimension=0, tiled=True
            ).astype(jnp.float32),
            lax.psum_scatter(
                layer_grads[4].astype(jnp.bfloat16), "fsdp", scatter_dimension=0, tiled=True
            ).astype(jnp.float32),
            lax.psum_scatter(
                layer_grads[5].astype(jnp.bfloat16), "fsdp", scatter_dimension=1, tiled=True
            ).astype(jnp.float32),
        )
    stacked = tuple(
        (
            jnp.stack([grad_list[layer_id][member] for layer_id in range(LAYERS)])
            for member in range(6)
        )
    )
    gains_grad, shifts_grad = (
        lax.psum_scatter(jnp.stack(gain_list), ("fsdp", "tp"), scatter_dimension=2, tiled=True),
        lax.psum_scatter(jnp.stack(shift_list), ("fsdp", "tp"), scatter_dimension=2, tiled=True),
    )
    return (
        out_rows,
        d_res,
        stacked[0],
        stacked[1],
        stacked[2],
        stacked[3],
        stacked[4],
        stacked[5],
        gains_grad,
        shifts_grad,
    )


def solution(mesh):
    in_specs = (
        P(("fsdp", "tp"), None),
        P(("fsdp", "tp"), None),
        P("fsdp", None),
        P(None, None, "fsdp", "tp"),
        P(None, None, ("tp", "fsdp")),
        P(None, "tp", "fsdp"),
        P(None, "fsdp", "tp"),
        P(None, ("tp", "fsdp")),
        P(None, "tp", "fsdp"),
        P(None, None, ("fsdp", "tp")),
        P(None, None, ("fsdp", "tp")),
    )
    out_specs = (
        P(("fsdp", "tp"), None),
        P(("fsdp", "tp"), None),
        P(None, None, "fsdp", "tp"),
        P(None, None, ("tp", "fsdp")),
        P(None, "tp", "fsdp"),
        P(None, "fsdp", "tp"),
        P(None, ("tp", "fsdp")),
        P(None, "tp", "fsdp"),
        P(None, None, ("fsdp", "tp")),
        P(None, None, ("fsdp", "tp")),
    )
    return jax.shard_map(body, mesh=mesh, in_specs=in_specs, out_specs=out_specs, check_vma=False)
```

profile of v0, /device:TPU:0, one launch (start us, length us, event | category | flops | bytes accessed | tf_op | source)
XLA Modules:
  0.0 1883.8 jit_solution(10463837423635150273)
XLA Ops:
  8.0 46.2 %all_gather.75 = f32[2,4,1024]{1,0,2:T(2,128)S(1)} all-gather(f32[2,4,32]{1,0,2:T(2,128)S(1)} %copy.99), channel_id=1, replica_groups=mesh['fsdp'=8,'tp'=4] {'fsdp','tp'}, dimensions={2}, use_global_device_ids=true | all-gather | bytes 33792 | tf_op jit(solution)/shard_map/all_gather | solution.py:152
  54.2 27.1 %slice_reduce_fusion = (f32[1024]{0:T(1024)S(1)}, f32[1024]{0:T(1024)S(1)}, f32[1024]{0:T(1024)S(1)}, f32[1024]{0:T(1024)S(1)}, f32[1024]{0:T(1024)S(1)}, /*inde...) fusion(f32[2,4,1024]{1,0,2:T(2,128)S(1)} %all_gather.75), kind=kLoop, calls=%fused_computation.148 | loop fusion | bytes 65536 | tf_op jit(solution)/shard_map/slice | solution.py:199
  81.5 40.1 %all_gather.74 = f32[2,2,1024]{1,0,2:T(2,128)S(1)} all-gather(f32[2,2,32]{1,0,2:T(2,128)S(1)} %copy.98), channel_id=1, replica_groups=mesh['fsdp'=8,'tp'=4] {'fsdp','tp'}, dimensions={2}, use_global_device_ids=true | all-gather | bytes 16896 | tf_op jit(solution)/shard_map/all_gather | solution.py:151
  121.6 26.0 %slice_reduce_fusion.2 = (f32[1024]{0:T(1024)S(1)}, f32[1024]{0:T(1024)S(1)}, f32[1024]{0:T(1024)S(1)}, f32[1024]{0:T(1024)S(1)}) fusion(f32[2,2,1024]{1,0,2:T(2,128)S(1)} %all_gather.74), kind=kLoop, calls=%fused_computation.150 | loop fusion | bytes 32768 | tf_op jit(solution)/shard_map/slice | solution.py:190
  150.4 30.7 %all-gather.1 = bf16[1,2,256]{1,0,2:T(2,128)(2,1)S(1)} all-gather(bf16[1,2,32]{1,0,2:T(2,128)(2,1)S(1)} %copy.160), channel_id=3, replica_groups=mesh['fsdp'=8,'tp'=4] {'fsdp'}, dimensions={2}, use_global_device_ids=true | all-gather | bytes 1152 | tf_op jit(solution)/shard_map/all_gather | solution.py:163
  181.2 31.3 %all-gather.7 = bf16[1,2,256]{1,0,2:T(2,128)(2,1)S(1)} all-gather(bf16[1,2,32]{1,0,2:T(2,128)(2,1)S(1)} %copy.162), channel_id=9, replica_groups=mesh['fsdp'=8,'tp'=4] {'fsdp'}, dimensions={2}, use_global_device_ids=true | all-gather | bytes 1152 | tf_op jit(solution)/shard_map/all_gather | solution.py:163
  212.5 3.6 fusion.121
  216.1 3.6 fusion.119
  219.8 27.0 %all-gather.2 = bf16[1,256,1024]{2,1,0:T(8,128)(2,1)S(1)} all-gather(bf16[1,256,128]{2,1,0:T(8,128)(2,1)S(1)} %get-tuple-element.119), channel_id=4, replica_groups=mesh['fsdp'=8,'tp'=4] {'fsdp'}, dimensions={2}, use_global_device_ids=true | all-gather | bytes 589824 | tf_op jit(solution)/shard_map/all_gather | solution.py:160
  247.1 2.7 fusion.54
  256.9 27.6 %reduce-scatter.41.cloned.1.call-done = f32[128,1024]{1,0:T(8,128)} async-done(((f32[512,1024]{1,0:T(8,128)}), f32[128,1024]{1,0:T(8,128)}) %reduce-scatter.41.cloned.1.call-update) | async-done | bytes 524304 | tf_op jit(solution)/shard_map/reduce_scatter | solution.py:106
  287.8 20.6 %all-gather.4 = bf16[1,1024]{1,0:T(2,128)(2,1)S(1)} all-gather(bf16[1,128]{1,0:T(2,128)(2,1)S(1)} %get-tuple-element.123), channel_id=6, replica_groups=mesh['fsdp'=8,'tp'=4] {'fsdp'}, dimensions={1}, use_global_device_ids=true | all-gather | bytes 2304 | tf_op jit(solution)/shard_map/all_gather | solution.py:164
  308.4 27.9 %all-gather.45.cloned.1.call-done = bf16[1,1024,1024]{2,1,0:T(8,128)(2,1)} async-done(((bf16[1,128,1024]{2,1,0:T(8,128)(2,1)}), bf16[1,1024,1024]{2,1,0:T(8,128)(2,1)}) %all-gather.45.cloned.1.call-update) | async-done | bytes 2097168 | tf_op jit(solution)/shard_map/all_gather | solution.py:161
  336.3 17.2 all-gather.29.cloned.1.call-done
  353.5 4.6 fusion.30
  358.1 48.3 %all-gather.47.cloned.1.call-done = bf16[1,1024,1024]{2,1,0:T(8,128)(2,1)} async-done(((bf16[1,1024,128]{2,1,0:T(8,128)(2,1)}), bf16[1,1024,1024]{2,1,0:T(8,128)(2,1)}) %all-gather.47.cloned.1.call-update) | async-done | bytes 2097168 | tf_op jit(solution)/shard_map/all_gather | solution.py:162
  406.4 5.1 fusion.26
  412.6 28.4 %reduce-scatter.43.cloned.1.call-done = f32[128,1024]{1,0:T(8,128)} async-done(((f32[512,1024]{1,0:T(8,128)}), f32[128,1024]{1,0:T(8,128)}) %reduce-scatter.43.cloned.1.call-update) | async-done | bytes 524304 | tf_op jit(solution)/shard_map/reduce_scatter | solution.py:106
  443.4 29.3 %all-gather.8 = bf16[1,256,1024]{2,1,0:T(8,128)(2,1)S(1)} all-gather(bf16[1,256,128]{2,1,0:T(8,128)(2,1)S(1)} %get-tuple-element.118), channel_id=10, replica_groups=mesh['fsdp'=8,'tp'=4] {'fsdp'}, dimensions={2}, use_global_device_ids=true | all-gather | bytes 589824 | tf_op jit(solution)/shard_map/all_gather | solution.py:160
  472.7 19.6 %all-gather.49.cloned.1.call-done = bf16[1,3,1024,256]{2,3,1,0:T(8,128)(2,1)} async-done(((bf16[1,3,128,256]{2,3,1,0:T(8,128)(2,1)}), bf16[1,3,1024,256]{2,3,1,0:T(8,128)(2,1)}) %all-gather.49.cloned.1.call-update) | async-done | bytes 1572880 | tf_op jit(solution)/shard_map/all_gather | solution.py:159
  492.3 17.1 all-gather.31.cloned.1.call-done
  509.4 2.7 fusion.57
  519.0 30.5 %reduce-scatter.45.cloned.1.call-done = f32[128,1024]{1,0:T(8,128)} async-done(((f32[512,1024]{1,0:T(8,128)}), f32[128,1024]{1,0:T(8,128)}) %reduce-scatter.45.cloned.1.call-update) | async-done | bytes 524304 | tf_op jit(solution)/shard_map/reduce_scatter | solution.py:106
  553.2 20.6 %all-gather.10 = bf16[1,1024]{1,0:T(2,128)(2,1)S(1)} all-gather(bf16[1,128]{1,0:T(2,128)(2,1)S(1)} %get-tuple-element.122), channel_id=12, replica_groups=mesh['fsdp'=8,'tp'=4] {'fsdp'}, dimensions={1}, use_global_device_ids=true | all-gather | bytes 2304 | tf_op jit(solution)/shard_map/all_gather | solution.py:164
  573.9 27.6 %all-gather.51.cloned.1.call-done = bf16[1,1024,1024]{2,1,0:T(8,128)(2,1)} async-done(((bf16[1,128,1024]{2,1,0:T(8,128)(2,1)}), bf16[1,1024,1024]{2,1,0:T(8,128)(2,1)}) %all-gather.51.cloned.1.call-update) | async-done | bytes 2097168 | tf_op jit(solution)/shard_map/all_gather | solution.py:161
  601.5 17.3 all-gather.33.cloned.1.call-done
  618.7 4.5 fusion.22
  623.2 13.8 all-gather.35.cloned.1.call-done
  637.0 52.9 %all-gather.53.cloned.1.call-done = bf16[1,1024,1024]{2,1,0:T(8,128)(2,1)} async-done(((bf16[1,1024,128]{2,1,0:T(8,128)(2,1)}), bf16[1,1024,1024]{2,1,0:T(8,128)(2,1)}) %all-gather.53.cloned.1.call-update) | async-done | bytes 2097168 | tf_op jit(solution)/shard_map/all_gather | solution.py:162
  689.9 5.2 fusion.151
  698.4 5.1 fusion.18
  703.9 17.5 reduce-scatter.49.cloned.1.call-done
  722.7 32.3 %reduce-scatter.47.cloned.1.call-done = f32[128,1024]{1,0:T(8,128)} async-done(((f32[512,1024]{1,0:T(8,128)}), f32[128,1024]{1,0:T(8,128)}) %reduce-scatter.47.cloned.1.call-update) | async-done | bytes 524304 | tf_op jit(solution)/shard_map/reduce_scatter | solution.py:106
  758.0 16.8 all-gather.37.cloned.1.call-done
  776.8 3.7 multiply_convert_fusion.1
  786.1 3.5 bitcast_convert_fusion.1
  789.7 24.9 %reduce-scatter.51.cloned.1.call-done = bf16[128,1024]{1,0:T(8,128)(2,1)} async-done(((bf16[512,1024]{1,0:T(8,128)(2,1)}), bf16[128,1024]{1,0:T(8,128)(2,1)}) %reduce-scatter.51.cloned.1.call-update) | async-done | bytes 262160 | tf_op jit(solution)/shard_map/reduce_scatter | solution.py:115
  817.8 16.8 all-gather.39.cloned.1.call-done
  834.6 5.2 fusion.152
  843.2 24.9 %reduce-scatter.53.cloned.1.call-done = bf16[128,1024]{1,0:T(8,128)(2,1)} async-done(((bf16[512,1024]{1,0:T(8,128)(2,1)}), bf16[128,1024]{1,0:T(8,128)(2,1)}) %reduce-scatter.53.cloned.1.call-update) | async-done | bytes 262160 | tf_op jit(solution)/shard_map/reduce_scatter | solution.py:115
  871.5 16.6 all-gather.41.cloned.1.call-done
  889.8 3.6 multiply_convert_fusion
  897.4 3.5 bitcast_convert_fusion
  901.0 3.5 convolution_convert_fusion
  909.9 3.6 fusion.53
  913.5 2.9 copy.141
  919.1 3.5 convolution_convert_fusion.1
  926.7 2.6 convolution_convert_fusion.2
  930.9 2.6 convolution_convert_fusion.3
  941.9 3.5 fusion.52
  945.4 2.9 copy.139
  951.2 47.0 %reduce-scatter.75.cloned.1.call-done = bf16[128,1024]{1,0:T(8,128)(2,1)} async-done(((bf16[1024,1024]{1,0:T(8,128)(2,1)}), bf16[128,1024]{1,0:T(8,128)(2,1)}) %reduce-scatter.75.cloned.1.call-update) | async-done | bytes 262160
  999.4 63.6 %reduce-scatter.67.cloned.1.call-done = bf16[32,2]{1,0:T(8,128)(2,1)} async-done(((bf16[256,2]{1,0:T(8,128)(2,1)}), bf16[32,2]{1,0:T(8,128)(2,1)}) %reduce-scatter.67.cloned.1.call-update) | async-done | bytes 144
  1063.8 64.8 %reduce-scatter.71.cloned.1.call-done = bf16[128,256]{1,0:T(8,128)(2,1)} async-done(((bf16[1024,256]{1,0:T(8,128)(2,1)}), bf16[128,256]{1,0:T(8,128)(2,1)}) %reduce-scatter.71.cloned.1.call-update) | async-done | bytes 65552
  1129.5 66.8 %reduce-scatter.63.cloned.1.call-done = bf16[128,768]{1,0:T(8,128)(2,1)} async-done(((bf16[1024,768]{1,0:T(8,128)(2,1)}), bf16[128,768]{1,0:T(8,128)(2,1)}) %reduce-scatter.63.cloned.1.call-update) | async-done | bytes 196624
  1197.5 19.1 %all-reduce.2 = (bf16[1024]{0:T(1024)(128)(2,1)S(1)}, bf16[1024]{0:T(1024)(128)(2,1)S(1)}) all-reduce(bf16[1024]{0:T(1024)(128)(2,1)S(1)} %get-tuple-element.138, bf16[1024]{0:T(1024)(128)(2,1)S(1)} %get-tuple-element.140), channel_id=31, replica_groups=mesh['fsdp'=8,'tp'=4] {'fsdp'}, use_global_device_ids=true, to_apply=%region_47.48.clone | all-reduce | flops 2048 | bytes 8192
  1217.4 43.6 %reduce-scatter.65.cloned.1.call-done = bf16[32,2]{1,0:T(8,128)(2,1)} async-done(((bf16[256,2]{1,0:T(8,128)(2,1)}), bf16[32,2]{1,0:T(8,128)(2,1)}) %reduce-scatter.65.cloned.1.call-update) | async-done | bytes 144
  1262.3 69.5 %reduce-scatter.73.cloned.1.call-done = bf16[128,1024]{1,0:T(8,128)(2,1)} async-done(((bf16[1024,1024]{1,0:T(8,128)(2,1)}), bf16[128,1024]{1,0:T(8,128)(2,1)}) %reduce-scatter.73.cloned.1.call-update) | async-done | bytes 262160
  1334.0 68.7 %reduce-scatter.59.cloned.1.call-done = bf16[128,1024]{1,0:T(8,128)(2,1)} async-done(((bf16[1024,1024]{1,0:T(8,128)(2,1)}), bf16[128,1024]{1,0:T(8,128)(2,1)}) %reduce-scatter.59.cloned.1.call-update) | async-done | bytes 262160 | tf_op jit(solution)/shard_map/reduce_scatter | solution.py:276
  1402.7 70.5 %reduce-scatter.57.cloned.1.call-done = bf16[128,1024]{1,0:T(8,128)(2,1)} async-done(((bf16[1024,1024]{1,0:T(8,128)(2,1)}), bf16[128,1024]{1,0:T(8,128)(2,1)}) %reduce-scatter.57.cloned.1.call-update) | async-done | bytes 262160 | tf_op jit(solution)/shard_map/reduce_scatter | solution.py:276
  1475.2 63.6 %reduce-scatter.69.cloned.1.call-done = bf16[128,256]{1,0:T(8,128)(2,1)} async-done(((bf16[1024,256]{1,0:T(8,128)(2,1)}), bf16[128,256]{1,0:T(8,128)(2,1)}) %reduce-scatter.69.cloned.1.call-update) | async-done | bytes 65552
  1541.5 134.2 %reduce-scatter.77.cloned.1.call-done = f32[32,4]{1,0:T(8,128)} async-done(((f32[1024,4]{1,0:T(8,128)}), f32[32,4]{1,0:T(8,128)}) %reduce-scatter.77.cloned.1.call-update) | async-done | bytes 528
  1677.1 132.3 %reduce-scatter.79.cloned.1.call-done = f32[32,8]{1,0:T(8,128)} async-done(((f32[1024,8]{1,0:T(8,128)}), f32[32,8]{1,0:T(8,128)}) %reduce-scatter.79.cloned.1.call-update) | async-done | bytes 1040
  1810.9 63.4 %reduce-scatter.61.cloned.1.call-done = bf16[128,768]{1,0:T(8,128)(2,1)} async-done(((bf16[1024,768]{1,0:T(8,128)(2,1)}), bf16[128,768]{1,0:T(8,128)(2,1)}) %reduce-scatter.61.cloned.1.call-update) | async-done | bytes 196624
  (296 shorter events, 101.8 us)
Async XLA Ops:
  7.2 239.9 %all-gather.27.cloned.1.call-start = ((), (), s32[]{:S(2)}) async-start(), calls=%async_computation.20 | async-start | bytes 1310720 | tf_op jit(solution)/shard_map/all_gather | solution.py:98
  54.2 27.2 %copy-start.32 = (f32[2,2,32]{2,1,0:T(2,128)S(1)}, f32[2,2,32]{2,1,0:T(2,128)}, u32[]{:S(2)}) copy-start(f32[2,2,32]{2,1,0:T(2,128)} %param.20) | copy-start | bytes 1540
  81.4 66.2 %copy-start.4 = (bf16[128,1024]{1,0:T(8,128)(2,1)S(1)}, bf16[128,1024]{1,0:T(8,128)(2,1)}, u32[]{:S(2)}) copy-start(bf16[128,1024]{1,0:T(8,128)(2,1)} %param.11) | copy-start | bytes 786436
  81.5 67.5 %copy-start.20 = (bf16[2,3,128,256]{3,2,1,0:T(8,128)(2,1)S(1)}, bf16[2,3,128,256]{3,2,1,0:T(8,128)(2,1)}, u32[]{:S(2)}) copy-start(bf16[2,3,128,256]{3,2,1,0:T(8,128)(2,1)} %param.14) | copy-start | bytes 1179652
  121.6 28.4 %copy-start.34 = (bf16[2,2,32]{2,1,0:T(2,128)(2,1)S(1)}, bf16[2,2,32]{2,1,0:T(2,128)(2,1)}, u32[]{:S(2)}) copy-start(bf16[2,2,32]{2,1,0:T(2,128)(2,1)} %param.15) | copy-start | bytes 772
  121.6 28.7 %copy-start.39 = (s32[1,8]{1,0:T(1,128)S(1)}, s32[1,8]{1,0:T(1,128)}, u32[]{:S(2)}) copy-start(s32[1,8]{1,0:T(1,128)} %param.13) | copy-start | bytes 100
  147.6 72.2 %copy-start.31 = (bf16[2,256,128]{2,1,0:T(8,128)(2,1)S(1)}, bf16[2,256,128]{2,1,0:T(8,128)(2,1)}, u32[]{:S(2)}) copy-start(bf16[2,256,128]{2,1,0:T(8,128)(2,1)} %param.16) | copy-start | bytes 393220
  149.0 98.1 %all-gather.43.cloned.1.call-start = ((), (), s32[]{:S(2)}) async-start(), calls=%async_computation.38 | async-start | bytes 1769472 | tf_op jit(solution)/shard_map/all_gather | solution.py:159
  149.9 134.6 %reduce-scatter.41.cloned.1.call-start = ((), (), s32[]{:S(2)}) async-start(), calls=%async_computation.21 | async-start | bytes 2621440 | tf_op jit(solution)/shard_map/reduce_scatter | solution.py:106
  246.9 7.2 copy-start.7
  250.9 1.9 copy-start
  254.1 1.9 copy-start.18
  255.9 30.9 %copy-start.19 = (bf16[2,1024,128]{2,1,0:T(8,128)(2,1)S(1)}, bf16[2,1024,128]{2,1,0:T(8,128)(2,1)}, u32[]{:S(2)}) copy-start(bf16[2,1024,128]{2,1,0:T(8,128)(2,1)} %param.19) | copy-start | bytes 1572868
  255.9 80.4 %all-gather.45.cloned.1.call-start = ((), (), s32[]{:S(2)}) async-start(), calls=%async_computation.39 | async-start | bytes 2359296 | tf_op jit(solution)/shard_map/all_gather | solution.py:161
  256.8 96.7 %all-gather.29.cloned.1.call-start = ((), (), s32[]{:S(2)}) async-start(), calls=%async_computation.22 | async-start | bytes 1310720 | tf_op jit(solution)/shard_map/all_gather | solution.py:98
  284.5 3.3 copy-start.33
  286.8 119.6 %all-gather.47.cloned.1.call-start = ((), (), s32[]{:S(2)}) async-start(), calls=%async_computation.40 | async-start | bytes 2359296 | tf_op jit(solution)/shard_map/all_gather | solution.py:162
  287.7 153.3 %reduce-scatter.43.cloned.1.call-start = ((), (), s32[]{:S(2)}) async-start(), calls=%async_computation.23 | async-start | bytes 2621440 | tf_op jit(solution)/shard_map/reduce_scatter | solution.py:106
  411.5 80.9 %all-gather.49.cloned.1.call-start = ((), (), s32[]{:S(2)}) async-start(), calls=%async_computation.41 | async-start | bytes 1769472 | tf_op jit(solution)/shard_map/all_gather | solution.py:159
  412.6 96.8 %all-gather.31.cloned.1.call-start = ((), (), s32[]{:S(2)}) async-start(), calls=%async_computation.24 | async-start | bytes 1310720 | tf_op jit(solution)/shard_map/all_gather | solution.py:98
  443.3 106.2 %reduce-scatter.45.cloned.1.call-start = ((), (), s32[]{:S(2)}) async-start(), calls=%async_computation.25 | async-start | bytes 2621440 | tf_op jit(solution)/shard_map/reduce_scatter | solution.py:106
  472.7 43.7 %copy-start.9 = (bf16[1,256,1024]{2,1,0:T(8,128)(2,1)}, bf16[1,256,1024]{2,1,0:T(8,128)(2,1)S(1)}, u32[]{:S(2)}) copy-start(bf16[1,256,1024]{2,1,0:T(8,128)(2,1)S(1)} %all-gather.8) | copy-start | bytes 1572868
  512.2 1.9 copy-start.29
  513.1 2.0 copy-start.2
  518.2 83.2 %all-gather.51.cloned.1.call-start = ((), (), s32[]{:S(2)}) async-start(), calls=%async_computation.42 | async-start | bytes 2359296 | tf_op jit(solution)/shard_map/all_gather | solution.py:161
  519.0 99.8 %all-gather.33.cloned.1.call-start = ((), (), s32[]{:S(2)}) async-start(), calls=%async_computation.26 | async-start | bytes 1310720 | tf_op jit(solution)/shard_map/all_gather | solution.py:98
  551.9 85.2 %all-gather.35.cloned.1.call-start = ((), (), s32[]{:S(2)}) async-start(), calls=%async_computation.28 | async-start | bytes 1310720 | tf_op jit(solution)/shard_map/all_gather | solution.py:102
  552.6 137.3 %all-gather.53.cloned.1.call-start = ((), (), s32[]{:S(2)}) async-start(), calls=%async_computation.43 | async-start | bytes 2359296 | tf_op jit(solution)/shard_map/all_gather | solution.py:162
  553.2 168.3 %reduce-scatter.49.cloned.1.call-start = ((), (), s32[]{:S(2)}) async-start(), calls=%async_computation.29 | async-start | bytes 1310720 | tf_op jit(solution)/shard_map/reduce_scatter | solution.py:115
  689.9 6.1 copy-start.36
  698.3 56.7 %reduce-scatter.47.cloned.1.call-start = ((), (), s32[]{:S(2)}) async-start(), calls=%async_computation.27 | async-start | bytes 2621440 | tf_op jit(solution)/shard_map/reduce_scatter | solution.py:106
  703.5 71.3 %all-gather.37.cloned.1.call-start = ((), (), s32[]{:S(2)}) async-start(), calls=%async_computation.30 | async-start | bytes 1310720 | tf_op jit(solution)/shard_map/all_gather | solution.py:102
  757.2 19.6 %copy-start.30 = (bf16[1,512,256]{1,2,0:T(8,128)(2,1)S(1)}, bf16[1,512,256]{1,2,0:T(8,128)(2,1)}, u32[]{:S(2)}) copy-start(bf16[1,512,256]{1,2,0:T(8,128)(2,1)} %copy-done.29) | copy-start | bytes 786436
  757.9 56.6 %reduce-scatter.51.cloned.1.call-start = ((), (), s32[]{:S(2)}) async-start(), calls=%async_computation.31 | async-start | bytes 1310720 | tf_op jit(solution)/shard_map/reduce_scatter | solution.py:115
  776.7 3.7 copy-start.6
  780.5 2.2 copy-start.3
  784.8 4.8 copy-start.23
  784.9 4.7 copy-start.25
  786.1 3.5 copy-start.26
  789.6 45.0 %all-gather.39.cloned.1.call-start = ((), (), s32[]{:S(2)}) async-start(), calls=%async_computation.32 | async-start | bytes 1310720 | tf_op jit(solution)/shard_map/all_gather | solution.py:102
  817.7 50.3 %reduce-scatter.53.cloned.1.call-start = ((), (), s32[]{:S(2)}) async-start(), calls=%async_computation.33 | async-start | bytes 1310720 | tf_op jit(solution)/shard_map/reduce_scatter | solution.py:115
  834.6 6.2 copy-start.35
  843.1 45.0 %copy-start.8 = (bf16[1,256,1024]{2,1,0:T(8,128)(2,1)S(1)}, bf16[1,256,1024]{2,1,0:T(8,128)(2,1)}, u32[]{:S(2)}) copy-start(bf16[1,256,1024]{2,1,0:T(8,128)(2,1)} %copy-done.7) | copy-start | bytes 1572868
  843.1 45.0 %copy-start.14 = (bf16[4,64,512]{2,1,0:T(8,128)(2,1)S(1)}, bf16[4,64,512]{2,1,0:T(8,128)(2,1)}, u32[]{:S(2)}) copy-start(bf16[4,64,512]{2,1,0:T(8,128)(2,1)} %copy-done.13) | copy-start | bytes 786436
  843.1 45.0 %all-gather.41.cloned.1.call-start = ((), (), s32[]{:S(2)}) async-start(), calls=%async_computation.34 | async-start | bytes 1310720 | tf_op jit(solution)/shard_map/all_gather | solution.py:102
  870.5 19.4 %copy-start.28 = (bf16[1,512,256]{1,2,0:T(8,128)(2,1)S(1)}, bf16[1,512,256]{1,2,0:T(8,128)(2,1)}, u32[]{:S(2)}) copy-start(bf16[1,512,256]{1,2,0:T(8,128)(2,1)} %copy-done.27) | copy-start | bytes 786436
  871.2 65.2 %reduce-scatter.55.cloned.1.call-start = ((), (), s32[]{:S(2)}) async-start(), calls=%async_computation.35 | async-start | bytes 1310720 | tf_op jit(solution)/shard_map/reduce_scatter | solution.py:115
  893.5 2.2 copy-start.1
  897.4 3.5 copy-start.21
  900.9 97.3 %reduce-scatter.75.cloned.1.call-start = ((), (), s32[]{:S(2)}) async-start(), calls=%async_computation.51 | async-start | bytes 2359296
  907.1 2.9 copy-start.24
  907.1 155.9 %reduce-scatter.67.cloned.1.call-start = ((), (), s32[]{:S(2)}) async-start(), calls=%async_computation.47 | async-start | bytes 73728
  908.1 220.5 %reduce-scatter.71.cloned.1.call-start = ((), (), s32[]{:S(2)}) async-start(), calls=%async_computation.49 | async-start | bytes 589824
  909.9 286.4 %reduce-scatter.63.cloned.1.call-start = ((), (), s32[]{:S(2)}) async-start(), calls=%async_computation.45 | async-start | bytes 1769472
  918.0 342.9 %reduce-scatter.65.cloned.1.call-start = ((), (), s32[]{:S(2)}) async-start(), calls=%async_computation.46 | async-start | bytes 73728
  919.0 412.8 %reduce-scatter.73.cloned.1.call-start = ((), (), s32[]{:S(2)}) async-start(), calls=%async_computation.50 | async-start | bytes 2359296
  925.2 477.5 %reduce-scatter.59.cloned.1.call-start = ((), (), s32[]{:S(2)}) async-start(), calls=%async_computation.37 | async-start | bytes 2359296 | tf_op jit(solution)/shard_map/reduce_scatter | solution.py:276
  929.4 543.7 %reduce-scatter.57.cloned.1.call-start = ((), (), s32[]{:S(2)}) async-start(), calls=%async_computation.36 | async-start | bytes 2359296 | tf_op jit(solution)/shard_map/reduce_scatter | solution.py:276
  933.6 605.2 %reduce-scatter.69.cloned.1.call-start = ((), (), s32[]{:S(2)}) async-start(), calls=%async_computation.48 | async-start | bytes 589824
  936.3 739.4 %reduce-scatter.77.cloned.1.call-start = ((), (), s32[]{:S(2)}) async-start(), calls=%async_computation.52 | async-start | bytes 540672
  939.7 2.2 copy-start.22
  939.7 869.8 %reduce-scatter.79.cloned.1.call-start = ((), (), s32[]{:S(2)}) async-start(), calls=%async_computation.53 | async-start | bytes 540672
  941.8 932.5 %reduce-scatter.61.cloned.1.call-start = ((), (), s32[]{:S(2)}) async-start(), calls=%async_computation.44 | async-start | bytes 1769472
  1331.8 208.7 %copy-start.12 = (bf16[128,1024]{1,0:T(8,128)(2,1)S(1)}, bf16[128,1024]{1,0:T(8,128)(2,1)}, u32[]{:S(2)}) copy-start(bf16[128,1024]{1,0:T(8,128)(2,1)} %reduce-scatter.55.cloned.1.call-done) | copy-start | bytes 786436
  (15 other events, 20.8 us)
Sparse Core Ops, SparseCore 0:
  149.1 14.1 all-gather.26
  165.9 45.5 all-gather.42
  256.0 28.3 reduce-scatter.40
  287.0 49.2 all-gather.44
  338.3 15.2 all-gather.28
  356.0 50.3 all-gather.46
  411.6 29.3 reduce-scatter.42
  443.6 48.6 all-gather.48
  494.5 14.8 all-gather.30
  518.3 31.1 reduce-scatter.44
  552.3 49.1 all-gather.50
  603.5 15.2 all-gather.32
  620.3 16.6 all-gather.34
  639.5 50.3 all-gather.52
  698.4 22.9 reduce-scatter.48
  723.8 31.1 reduce-scatter.46
  758.1 16.7 all-gather.36
  789.7 24.7 reduce-scatter.50
  817.9 16.7 all-gather.38
  843.2 24.7 reduce-scatter.52
  871.3 16.6 all-gather.40
  901.0 24.8 reduce-scatter.54
  929.4 68.7 reduce-scatter.74
  1001.5 61.4 reduce-scatter.66
  1066.9 61.5 reduce-scatter.70
  1131.8 64.4 reduce-scatter.62
  1199.6 61.3 reduce-scatter.64
  1264.4 67.2 reduce-scatter.72
  1335.3 67.3 reduce-scatter.58
  1406.0 67.0 reduce-scatter.56
  1477.0 61.6 reduce-scatter.68
  1541.0 134.6 reduce-scatter.76
  1677.7 131.6 reduce-scatter.78
  1812.9 61.3 reduce-scatter.60
where the time goes:
time: 1890 us; the launch traced here: 1880 us
  waiting for transfers between devices  1370 us (72%)
  blocking collectives  265 us (14%)
  local copies, waits for them, and re-layouts  105 us (6%)
  matrix products  91.5 us (5%)
  other arithmetic  35.7 us (2%)
    unnamed x44, waiting for transfers between devices  751 us
    reduce_scatter x2, waiting for transfers between devices, body(): lax.psum_scatter(layer_grads[3].astype(jnp.bfloat16), 'fsdp', scatter_dim...  139 us
    reduce_scatter x4, waiting for transfers between devices, sum_branch(): lax.psum_scatter(partial_fn(jnp.int32(0), tok_rows * lax.axis_size('tp'))...  119 us
    all_gather x2, waiting for transfers between devices, body(): lax.all_gather(proj_weight[layer_id], 'fsdp', axis=1, tiled=True)  101 us
    reduce_scatter x4, waiting for transfers between devices, sum_inputs(): lax.psum_scatter(partial_fn(jnp.int32(0), tok_rows * lax.axis_size('tp'))...  67.3 us
    all_gather x4, waiting for transfers between devices, gather_grads(): return lax.all_gather(values, 'tp', axis=0, tiled=True)  64.1 us
    all_gather x2, blocking collectives, body(): lax.all_gather(qv_bias[layer_id], 'fsdp', axis=1, tiled=True)  62 us
    all_gather x2, blocking collectives, body(): lax.all_gather(out_weight[layer_id], 'fsdp', axis=1, tiled=True)  56.4 us
  transfers between devices with their start and end apart: 34, of which 31 were waited for; matrix products, arithmetic and copies ran while one was open for 5% of the time, Pallas kernels for 0%

commit v1 on v0

--- a/solution.py
+++ b/solution.py
@@ -6,6 +6,18 @@
 HEAD_DIM = 64
 LAYERS = 2
 eps_norm = 1e-05
+
+
+def collect(x, axis, dim):
+    ways, here, turn = (lax.axis_size(axis), lax.axis_index(axis), x.shape[dim])
+    line, have = (x, 1)
+    while have < ways:
+        line = jnp.concatenate(
+            [line, lax.ppermute(line, axis, [(d, (d - have) % ways) for d in range(ways)])],
+            axis=dim,
+        )
+        have = 2 * have
+    return jnp.roll(line, here * turn, axis=dim)
 
 
 def norm_stats(values):
@@ -159,7 +171,7 @@
             lax.all_gather(qkv_weight[layer_id], "fsdp", axis=1, tiled=True),
             lax.all_gather(out_weight[layer_id], "fsdp", axis=1, tiled=True),
             lax.all_gather(fc_weight[layer_id], "fsdp", axis=0, tiled=True),
-            lax.all_gather(proj_weight[layer_id], "fsdp", axis=1, tiled=True),
+            collect(proj_weight[layer_id], "fsdp", 1),
             lax.all_gather(qv_bias[layer_id], "fsdp", axis=1, tiled=True),
             lax.all_gather(fc_bias[layer_id], "fsdp", axis=0, tiled=True),
         )

time: 1890 us -> 1970 us (1.042)
  waiting for transfers between devices: 1370 us -> 1410 us
  blocking collectives: 265 us -> 286 us
    ppermute x0 -> x6, waiting for transfers between devices: none -> 64.6 us  [collect(): lax.ppermute(line, axis, [(d, (d - have) % ways) for d in range(ways)])]
    unnamed x126 -> x134, local copies, waits for them, and re-layouts: 47.3 us -> 48.4 us
  transfers between devices with their start and end apart: 34 -> 40, of which waited for: 31 -> 32; matrix products, arithmetic and copies ran while one was open for 5% -> 5% of each run, Pallas kernels for 0% -> 0%
where the time goes in v1:
time: 1970 us; the launch traced here: 1960 us
  waiting for transfers between devices  1410 us (72%)
  blocking collectives  286 us (15%)
  local copies, waits for them, and re-layouts  107 us (5%)
  matrix products  94.2 us (5%)
  other arithmetic  37.9 us (2%)
    unnamed x44, waiting for transfers between devices  752 us
    reduce_scatter x2, waiting for transfers between devices, body(): lax.psum_scatter(layer_grads[3].astype(jnp.bfloat16), 'fsdp', scatter_dim...  140 us
    reduce_scatter x4, waiting for transfers between devices, sum_branch(): lax.psum_scatter(partial_fn(jnp.int32(0), tok_rows * lax.axis_size('tp'))...  118 us
    all_gather x2, waiting for transfers between devices, body(): lax.all_gather(proj_weight[layer_id], 'fsdp', axis=1, tiled=True)  102 us
    ppermute x6, waiting for transfers between devices, collect(): lax.ppermute(line, axis, [(d, (d - have) % ways) for d in range(ways)])  64.6 us
    all_gather x4, waiting for transfers between devices, gather_grads(): return lax.all_gather(values, 'tp', axis=0, tiled=True)  63.9 us
    all_gather x2, blocking collectives, body(): lax.all_gather(qv_bias[layer_id], 'fsdp', axis=1, tiled=True)  62 us
    all_gather x2, blocking collectives, body(): lax.all_gather(fc_bias[layer_id], 'fsdp', axis=0, tiled=True)  60.4 us
  transfers between devices with their start and end apart: 40, of which 32 were waited for; matrix products, arithmetic and copies ran while one was open for 5% of the time, Pallas kernels for 0%

profile of v1, /device:TPU:0, one launch (start us, length us, event | category | flops | bytes accessed | tf_op | source)
XLA Modules:
  0.0 1963.6 jit_solution(6432219855208353484)
XLA Ops:
  8.0 46.2 %all_gather.73 = f32[2,4,1024]{1,0,2:T(2,128)S(1)} all-gather(f32[2,4,32]{1,0,2:T(2,128)S(1)} %copy.99), channel_id=1, replica_groups=mesh['fsdp'=8,'tp'=4] {'fsdp','tp'}, dimensions={2}, use_global_device_ids=true | all-gather | bytes 33792 | tf_op jit(solution)/shard_map/all_gather | solution.py:164
  54.2 27.3 %slice_reduce_fusion = (f32[1024]{0:T(1024)S(1)}, f32[1024]{0:T(1024)S(1)}, f32[1024]{0:T(1024)S(1)}, f32[1024]{0:T(1024)S(1)}, f32[1024]{0:T(1024)S(1)}, /*inde...) fusion(f32[2,4,1024]{1,0,2:T(2,128)S(1)} %all_gather.73), kind=kLoop, calls=%fused_computation.178 | loop fusion | bytes 65536 | tf_op jit(solution)/shard_map/slice | solution.py:211
  81.7 40.2 %all_gather.72 = f32[2,2,1024]{1,0,2:T(2,128)S(1)} all-gather(f32[2,2,32]{1,0,2:T(2,128)S(1)} %copy.98), channel_id=1, replica_groups=mesh['fsdp'=8,'tp'=4] {'fsdp','tp'}, dimensions={2}, use_global_device_ids=true | all-gather | bytes 16896 | tf_op jit(solution)/shard_map/all_gather | solution.py:163
  121.8 26.0 %slice_reduce_fusion.2 = (f32[1024]{0:T(1024)S(1)}, f32[1024]{0:T(1024)S(1)}, f32[1024]{0:T(1024)S(1)}, f32[1024]{0:T(1024)S(1)}) fusion(f32[2,2,1024]{1,0,2:T(2,128)S(1)} %all_gather.72), kind=kLoop, calls=%fused_computation.180 | loop fusion | bytes 32768 | tf_op jit(solution)/shard_map/slice | solution.py:202
  151.4 30.6 %all-gather.6 = bf16[1,2,256]{1,0,2:T(2,128)(2,1)S(1)} all-gather(bf16[1,2,32]{1,0,2:T(2,128)(2,1)S(1)} %copy.162), channel_id=8, replica_groups=mesh['fsdp'=8,'tp'=4] {'fsdp'}, dimensions={2}, use_global_device_ids=true | all-gather | bytes 1152 | tf_op jit(solution)/shard_map/all_gather | solution.py:175
  182.0 31.4 %all-gather.1 = bf16[1,2,256]{1,0,2:T(2,128)(2,1)S(1)} all-gather(bf16[1,2,32]{1,0,2:T(2,128)(2,1)S(1)} %copy.160), channel_id=3, replica_groups=mesh['fsdp'=8,'tp'=4] {'fsdp'}, dimensions={2}, use_global_device_ids=true | all-gather | bytes 1152 | tf_op jit(solution)/shard_map/all_gather | solution.py:175
  213.5 3.6 fusion.133
  217.1 3.6 fusion.135
  220.8 27.1 %all-gather.2 = bf16[1,256,1024]{2,1,0:T(8,128)(2,1)S(1)} all-gather(bf16[1,256,128]{2,1,0:T(8,128)(2,1)S(1)} %get-tuple-element.122), channel_id=4, replica_groups=mesh['fsdp'=8,'tp'=4] {'fsdp'}, dimensions={2}, use_global_device_ids=true | all-gather | bytes 589824 | tf_op jit(solution)/shard_map/all_gather | solution.py:172
  248.2 2.7 fusion.68
  258.9 28.9 %reduce-scatter.41.cloned.1.call-done = f32[128,1024]{1,0:T(8,128)} async-done(((f32[512,1024]{1,0:T(8,128)}), f32[128,1024]{1,0:T(8,128)}) %reduce-scatter.41.cloned.1.call-update) | async-done | bytes 524304 | tf_op jit(solution)/shard_map/reduce_scatter | solution.py:118
  290.3 3.4 collective-permute-start.1
  293.7 19.0 collective-permute-done.1
  313.4 37.0 %all-gather.4 = bf16[1,1024]{1,0:T(2,128)(2,1)S(1)} all-gather(bf16[1,128]{1,0:T(2,128)(2,1)S(1)} %get-tuple-element.126), channel_id=6, replica_groups=mesh['fsdp'=8,'tp'=4] {'fsdp'}, dimensions={1}, use_global_device_ids=true | all-gather | bytes 2304 | tf_op jit(solution)/shard_map/all_gather | solution.py:176
  350.4 21.9 %all-gather.45.cloned.1.call-done = bf16[1,1024,1024]{2,1,0:T(8,128)(2,1)} async-done(((bf16[1,128,1024]{2,1,0:T(8,128)(2,1)}), bf16[1,1024,1024]{2,1,0:T(8,128)(2,1)}) %all-gather.45.cloned.1.call-update) | async-done | bytes 2097168 | tf_op jit(solution)/shard_map/all_gather | solution.py:173
  372.3 22.5 %all-gather.29.cloned.1.call-done = bf16[512,1024]{1,0:T(8,128)(2,1)} async-done(((bf16[128,1024]{1,0:T(8,128)(2,1)}), bf16[512,1024]{1,0:T(8,128)(2,1)}) %all-gather.29.cloned.1.call-update) | async-done | bytes 1048592 | tf_op jit(solution)/shard_map/all_gather | solution.py:110
  394.7 3.2 fusion.40
  399.4 6.9 fusion.42
  408.1 29.5 %reduce-scatter.43.cloned.1.call-done = f32[128,1024]{1,0:T(8,128)} async-done(((f32[512,1024]{1,0:T(8,128)}), f32[128,1024]{1,0:T(8,128)}) %reduce-scatter.43.cloned.1.call-update) | async-done | bytes 524304 | tf_op jit(solution)/shard_map/reduce_scatter | solution.py:118
  440.0 31.1 %all-gather.7 = bf16[1,256,1024]{2,1,0:T(8,128)(2,1)} all-gather(bf16[1,256,128]{2,1,0:T(8,128)(2,1)S(1)} %get-tuple-element.121), channel_id=9, replica_groups=mesh['fsdp'=8,'tp'=4] {'fsdp'}, dimensions={2}, use_global_device_ids=true | all-gather | bytes 589824 | tf_op jit(solution)/shard_map/all_gather | solution.py:172
  471.1 16.2 all-gather.47.cloned.1.call-done
  487.3 17.0 all-gather.31.cloned.1.call-done
  513.8 30.7 %reduce-scatter.45.cloned.1.call-done = f32[128,1024]{1,0:T(8,128)} async-done(((f32[512,1024]{1,0:T(8,128)}), f32[128,1024]{1,0:T(8,128)}) %reduce-scatter.45.cloned.1.call-update) | async-done | bytes 524304 | tf_op jit(solution)/shard_map/reduce_scatter | solution.py:118
  548.2 4.3 collective-permute-start.3
  552.5 23.4 %all-gather.9 = bf16[1,1024]{1,0:T(2,128)(2,1)S(1)} all-gather(bf16[1,128]{1,0:T(2,128)(2,1)S(1)} %get-tuple-element.125), channel_id=11, replica_groups=mesh['fsdp'=8,'tp'=4] {'fsdp'}, dimensions={1}, use_global_device_ids=true | all-gather | bytes 2304 | tf_op jit(solution)/shard_map/all_gather | solution.py:176
  577.2 22.9 %all-gather.49.cloned.1.call-done = bf16[1,1024,1024]{2,1,0:T(8,128)(2,1)} async-done(((bf16[1,128,1024]{2,1,0:T(8,128)(2,1)}), bf16[1,1024,1024]{2,1,0:T(8,128)(2,1)}) %all-gather.49.cloned.1.call-update) | async-done | bytes 2097168 | tf_op jit(solution)/shard_map/all_gather | solution.py:173
  600.1 19.0 all-gather.33.cloned.1.call-done
  619.1 4.5 fusion.36
  623.7 13.6 all-gather.35.cloned.1.call-done
  637.3 53.0 %all-gather.51.cloned.1.call-done = bf16[1,1024,1024]{2,1,0:T(8,128)(2,1)} async-done(((bf16[1,1024,128]{2,1,0:T(8,128)(2,1)}), bf16[1,1024,1024]{2,1,0:T(8,128)(2,1)}) %all-gather.51.cloned.1.call-update) | async-done | bytes 2097168 | tf_op jit(solution)/shard_map/all_gather | solution.py:226
  690.3 5.2 fusion.169
  701.7 45.6 %collective-permute-done.5 = bf16[1024,512]{1,0:T(8,128)(2,1)S(1)} collective-permute-done((bf16[1024,512]{1,0:T(8,128)(2,1)S(1)}, bf16[1024,512]{1,0:T(8,128)(2,1)S(1)}, u32[]{:S(2)}, u32[]{:S(2)}) %collective-permute-start.5) | collective-permute-done | bytes 1048608 | tf_op jit(solution)/shard_map/ppermute | solution.py:16
  747.3 6.7 fusion.44
  755.4 29.3 %reduce-scatter.47.cloned.1.call-done = f32[128,1024]{1,0:T(8,128)} async-done(((f32[512,1024]{1,0:T(8,128)}), f32[128,1024]{1,0:T(8,128)}) %reduce-scatter.47.cloned.1.call-update) | async-done | bytes 524304 | tf_op jit(solution)/shard_map/reduce_scatter | solution.py:118
  787.8 16.6 all-gather.37.cloned.1.call-done
  806.4 4.3 fusion.162
  815.6 3.5 bitcast_convert_fusion.1
  819.8 24.3 %reduce-scatter.51.cloned.1.call-done = bf16[128,1024]{1,0:T(8,128)(2,1)} async-done(((bf16[512,1024]{1,0:T(8,128)(2,1)}), bf16[128,1024]{1,0:T(8,128)(2,1)}) %reduce-scatter.51.cloned.1.call-update) | async-done | bytes 262160 | tf_op jit(solution)/shard_map/reduce_scatter | solution.py:127
  847.4 49.0 %all-gather.53.cloned.1.call-done = bf16[1,1024,1024]{2,1,0:T(8,128)(2,1)} async-done(((bf16[1,1024,128]{2,1,0:T(8,128)(2,1)}), bf16[1,1024,1024]{2,1,0:T(8,128)(2,1)}) %all-gather.53.cloned.1.call-update) | async-done | bytes 2097168 | tf_op jit(solution)/shard_map/all_gather | solution.py:226
  896.4 17.0 all-gather.39.cloned.1.call-done
  913.4 5.2 fusion.170
  921.9 24.9 %reduce-scatter.53.cloned.1.call-done = bf16[128,1024]{1,0:T(8,128)(2,1)} async-done(((bf16[512,1024]{1,0:T(8,128)(2,1)}), bf16[128,1024]{1,0:T(8,128)(2,1)}) %reduce-scatter.53.cloned.1.call-update) | async-done | bytes 262160 | tf_op jit(solution)/shard_map/reduce_scatter | solution.py:127
  950.3 16.6 all-gather.41.cloned.1.call-done
  968.6 3.6 fusion.160
  975.5 3.5 bitcast_convert_fusion
  979.1 3.5 convolution_convert_fusion
  988.1 3.6 fusion.67
  991.6 2.9 copy.141
  997.2 3.5 convolution_convert_fusion.1
  1020.0 3.5 fusion.66
  1023.5 2.9 copy.139
  1029.3 47.3 %reduce-scatter.75.cloned.1.call-done = bf16[128,1024]{1,0:T(8,128)(2,1)} async-done(((bf16[1024,1024]{1,0:T(8,128)(2,1)}), bf16[128,1024]{1,0:T(8,128)(2,1)}) %reduce-scatter.75.cloned.1.call-update) | async-done | bytes 262160
  1077.8 63.6 %reduce-scatter.67.cloned.1.call-done = bf16[32,2]{1,0:T(8,128)(2,1)} async-done(((bf16[256,2]{1,0:T(8,128)(2,1)}), bf16[32,2]{1,0:T(8,128)(2,1)}) %reduce-scatter.67.cloned.1.call-update) | async-done | bytes 144
  1142.2 64.9 %reduce-scatter.71.cloned.1.call-done = bf16[128,256]{1,0:T(8,128)(2,1)} async-done(((bf16[1024,256]{1,0:T(8,128)(2,1)}), bf16[128,256]{1,0:T(8,128)(2,1)}) %reduce-scatter.71.cloned.1.call-update) | async-done | bytes 65552
  1208.0 66.9 %reduce-scatter.63.cloned.1.call-done = bf16[128,768]{1,0:T(8,128)(2,1)} async-done(((bf16[1024,768]{1,0:T(8,128)(2,1)}), bf16[128,768]{1,0:T(8,128)(2,1)}) %reduce-scatter.63.cloned.1.call-update) | async-done | bytes 196624
  1276.1 19.2 all-reduce.2
  1296.0 44.0 %reduce-scatter.65.cloned.1.call-done = bf16[32,2]{1,0:T(8,128)(2,1)} async-done(((bf16[256,2]{1,0:T(8,128)(2,1)}), bf16[32,2]{1,0:T(8,128)(2,1)}) %reduce-scatter.65.cloned.1.call-update) | async-done | bytes 144
  1341.4 69.5 %reduce-scatter.73.cloned.1.call-done = bf16[128,1024]{1,0:T(8,128)(2,1)} async-done(((bf16[1024,1024]{1,0:T(8,128)(2,1)}), bf16[128,1024]{1,0:T(8,128)(2,1)}) %reduce-scatter.73.cloned.1.call-update) | async-done | bytes 262160
  1412.0 69.7 %reduce-scatter.59.cloned.1.call-done = bf16[128,1024]{1,0:T(8,128)(2,1)} async-done(((bf16[1024,1024]{1,0:T(8,128)(2,1)}), bf16[128,1024]{1,0:T(8,128)(2,1)}) %reduce-scatter.59.cloned.1.call-update) | async-done | bytes 262160 | tf_op jit(solution)/shard_map/reduce_scatter | solution.py:288
  1481.7 70.7 %reduce-scatter.57.cloned.1.call-done = bf16[128,1024]{1,0:T(8,128)(2,1)} async-done(((bf16[1024,1024]{1,0:T(8,128)(2,1)}), bf16[128,1024]{1,0:T(8,128)(2,1)}) %reduce-scatter.57.cloned.1.call-update) | async-done | bytes 262160 | tf_op jit(solution)/shard_map/reduce_scatter | solution.py:288
  1555.5 62.6 %reduce-scatter.69.cloned.1.call-done = bf16[128,256]{1,0:T(8,128)(2,1)} async-done(((bf16[1024,256]{1,0:T(8,128)(2,1)}), bf16[128,256]{1,0:T(8,128)(2,1)}) %reduce-scatter.69.cloned.1.call-update) | async-done | bytes 65552
  1620.8 134.2 %reduce-scatter.77.cloned.1.call-done = f32[32,4]{1,0:T(8,128)} async-done(((f32[1024,4]{1,0:T(8,128)}), f32[32,4]{1,0:T(8,128)}) %reduce-scatter.77.cloned.1.call-update) | async-done | bytes 528
  1756.5 132.4 %reduce-scatter.79.cloned.1.call-done = f32[32,8]{1,0:T(8,128)} async-done(((f32[1024,8]{1,0:T(8,128)}), f32[32,8]{1,0:T(8,128)}) %reduce-scatter.79.cloned.1.call-update) | async-done | bytes 1040
  1890.4 63.6 %reduce-scatter.61.cloned.1.call-done = bf16[128,768]{1,0:T(8,128)(2,1)} async-done(((bf16[1024,768]{1,0:T(8,128)(2,1)}), bf16[128,768]{1,0:T(8,128)(2,1)}) %reduce-scatter.61.cloned.1.call-update) | async-done | bytes 196624
  (320 shorter events, 116.5 us)
Async XLA Ops:
  7.2 241.0 %all-gather.27.cloned.1.call-start = ((), (), s32[]{:S(2)}) async-start(), calls=%async_computation.20 | async-start | bytes 1310720 | tf_op jit(solution)/shard_map/all_gather | solution.py:110
  54.2 27.4 %copy-start.34 = (f32[2,2,32]{2,1,0:T(2,128)S(1)}, f32[2,2,32]{2,1,0:T(2,128)}, u32[]{:S(2)}) copy-start(f32[2,2,32]{2,1,0:T(2,128)} %param.22) | copy-start | bytes 1540
  81.6 66.3 %copy-start.4 = (bf16[128,1024]{1,0:T(8,128)(2,1)S(1)}, bf16[128,1024]{1,0:T(8,128)(2,1)}, u32[]{:S(2)}) copy-start(bf16[128,1024]{1,0:T(8,128)(2,1)} %param.13) | copy-start | bytes 786436
  81.7 67.6 %copy-start.23 = (bf16[2,3,128,256]{3,2,1,0:T(8,128)(2,1)S(1)}, bf16[2,3,128,256]{3,2,1,0:T(8,128)(2,1)}, u32[]{:S(2)}) copy-start(bf16[2,3,128,256]{3,2,1,0:T(8,128)(2,1)} %param.16) | copy-start | bytes 1179652
  121.8 29.0 %copy-start.36 = (bf16[2,2,32]{2,1,0:T(2,128)(2,1)S(1)}, bf16[2,2,32]{2,1,0:T(2,128)(2,1)}, u32[]{:S(2)}) copy-start(bf16[2,2,32]{2,1,0:T(2,128)(2,1)} %param.17) | copy-start | bytes 772
  121.8 29.3 %copy-start.41 = (s32[1,8]{1,0:T(1,128)S(1)}, s32[1,8]{1,0:T(1,128)}, u32[]{:S(2)}) copy-start(s32[1,8]{1,0:T(1,128)} %param.15) | copy-start | bytes 100
  147.9 72.9 %copy-start.33 = (bf16[2,256,128]{2,1,0:T(8,128)(2,1)S(1)}, bf16[2,256,128]{2,1,0:T(8,128)(2,1)}, u32[]{:S(2)}) copy-start(bf16[2,256,128]{2,1,0:T(8,128)(2,1)} %param.18) | copy-start | bytes 393220
  149.2 99.0 %all-gather.43.cloned.1.call-start = ((), (), s32[]{:S(2)}) async-start(), calls=%async_computation.38 | async-start | bytes 1769472 | tf_op jit(solution)/shard_map/all_gather | solution.py:171
  150.8 137.0 %reduce-scatter.41.cloned.1.call-start = ((), (), s32[]{:S(2)}) async-start(), calls=%async_computation.21 | async-start | bytes 2621440 | tf_op jit(solution)/shard_map/reduce_scatter | solution.py:118
  247.9 7.2 copy-start.7
  257.0 115.3 %all-gather.45.cloned.1.call-start = ((), (), s32[]{:S(2)}) async-start(), calls=%async_computation.39 | async-start | bytes 2359296 | tf_op jit(solution)/shard_map/all_gather | solution.py:173
  257.9 136.8 %all-gather.29.cloned.1.call-start = ((), (), s32[]{:S(2)}) async-start(), calls=%async_computation.22 | async-start | bytes 1310720 | tf_op jit(solution)/shard_map/all_gather | solution.py:110
  258.9 31.3 %collective-permute-start = (bf16[1024,128]{1,0:T(8,128)(2,1)S(1)}, bf16[1024,128]{1,0:T(8,128)(2,1)S(1)}, u32[]{:S(2)}, u32[]{:S(2)}) collective-permute-start(bf16[1024,128]{1,0:T(8,128)(2,1)S(1)} %get-tuple-element.112), channel_id=1, source_target_pairs={{0,28},{4,0},{8,4},{12,8},{16,12},{20,16},{24,20},{28,24},{1,29},{... | collective-permute-start | bytes 786440 | tf_op jit(solution)/shard_map/ppermute | solution.py:16
  289.3 24.2 %copy-start.35 = (bf16[2,128]{1,0:T(2,128)(2,1)S(1)}, bf16[2,128]{1,0:T(2,128)(2,1)}, u32[]{:S(2)}) copy-start(bf16[2,128]{1,0:T(2,128)(2,1)} %param.20) | copy-start | bytes 1540
  290.2 147.5 %reduce-scatter.43.cloned.1.call-start = ((), (), s32[]{:S(2)}) async-start(), calls=%async_computation.23 | async-start | bytes 2621440 | tf_op jit(solution)/shard_map/reduce_scatter | solution.py:118
  290.3 22.3 %collective-permute-start.1 = (bf16[1024,256]{1,0:T(8,128)(2,1)S(1)}, bf16[1024,256]{1,0:T(8,128)(2,1)S(1)}, u32[]{:S(2)}, u32[]{:S(2)}) collective-permute-start(bf16[1024,256]{1,0:T(8,128)(2,1)S(1)} %pad_maximum_fusion.4), channel_id=1, source_target_pairs={{0,24},{4,28},{8,0},{12,4},{16,8},{20,12},{24,16},{28,20},{1,25},{... | collective-permute-start | bytes 1572872 | tf_op jit(solution)/shard_map/ppermute | solution.py:16
  312.7 85.2 %collective-permute-start.2 = (bf16[1024,512]{1,0:T(8,128)(2,1)S(1)}, bf16[1024,512]{1,0:T(8,128)(2,1)}, u32[]{:S(2)}, u32[]{:S(2)}) collective-permute-start(bf16[1024,512]{1,0:T(8,128)(2,1)S(1)} %pad_maximum_fusion), channel_id=1, source_target_pairs={{0,16},{4,20},{8,24},{12,28},{16,0},{20,4},{24,8},{28,12},{1,17},{... | collective-permute-start | bytes 3145736 | tf_op jit(solution)/shard_map/ppermute | solution.py:16
  394.7 4.6 copy-start.22
  406.3 81.0 %all-gather.47.cloned.1.call-start = ((), (), s32[]{:S(2)}) async-start(), calls=%async_computation.40 | async-start | bytes 1769472 | tf_op jit(solution)/shard_map/all_gather | solution.py:171
  408.0 96.3 %all-gather.31.cloned.1.call-start = ((), (), s32[]{:S(2)}) async-start(), calls=%async_computation.24 | async-start | bytes 1310720 | tf_op jit(solution)/shard_map/all_gather | solution.py:110
  439.9 104.6 %reduce-scatter.45.cloned.1.call-start = ((), (), s32[]{:S(2)}) async-start(), calls=%async_computation.25 | async-start | bytes 2621440 | tf_op jit(solution)/shard_map/reduce_scatter | solution.py:118
  513.2 86.9 %all-gather.49.cloned.1.call-start = ((), (), s32[]{:S(2)}) async-start(), calls=%async_computation.41 | async-start | bytes 2359296 | tf_op jit(solution)/shard_map/all_gather | solution.py:173
  513.8 105.3 %all-gather.33.cloned.1.call-start = ((), (), s32[]{:S(2)}) async-start(), calls=%async_computation.26 | async-start | bytes 1310720 | tf_op jit(solution)/shard_map/all_gather | solution.py:110
  546.8 90.5 %all-gather.35.cloned.1.call-start = ((), (), s32[]{:S(2)}) async-start(), calls=%async_computation.28 | async-start | bytes 1310720 | tf_op jit(solution)/shard_map/all_gather | solution.py:114
  547.4 142.9 %all-gather.51.cloned.1.call-start = ((), (), s32[]{:S(2)}) async-start(), calls=%async_computation.42 | async-start | bytes 2359296 | tf_op jit(solution)/shard_map/all_gather | solution.py:226
  548.1 206.0 %reduce-scatter.49.cloned.1.call-start = ((), (), s32[]{:S(2)}) async-start(), calls=%async_computation.29 | async-start | bytes 1310720 | tf_op jit(solution)/shard_map/reduce_scatter | solution.py:127
  548.2 27.7 %collective-permute-start.3 = (bf16[1024,128]{1,0:T(8,128)(2,1)S(1)}, bf16[1024,128]{1,0:T(8,128)(2,1)S(1)}, u32[]{:S(2)}, u32[]{:S(2)}) collective-permute-start(bf16[1024,128]{1,0:T(8,128)(2,1)S(1)} %get-tuple-element.113), channel_id=1, source_target_pairs={{0,28},{4,0},{8,4},{12,8},{16,12},{20,16},{24,20},{28,24},{1,29},{... | collective-permute-start | bytes 786440 | tf_op jit(solution)/shard_map/ppermute | solution.py:16
  576.8 122.0 %collective-permute-start.4 = (bf16[1024,256]{1,0:T(8,128)(2,1)}, bf16[1024,256]{1,0:T(8,128)(2,1)}, u32[]{:S(2)}, u32[]{:S(2)}) collective-permute-start(bf16[1024,256]{1,0:T(8,128)(2,1)} %pad_maximum_fusion.5), channel_id=1, source_target_pairs={{0,24},{4,28},{8,0},{12,4},{16,8},{20,12},{24,16},{28,20},{1,25},{... | collective-permute-start | bytes 1572872 | tf_op jit(solution)/shard_map/ppermute | solution.py:16
  690.3 6.1 copy-start.38
  698.7 85.9 %reduce-scatter.47.cloned.1.call-start = ((), (), s32[]{:S(2)}) async-start(), calls=%async_computation.27 | async-start | bytes 2621440 | tf_op jit(solution)/shard_map/reduce_scatter | solution.py:118
  698.8 48.5 %copy-start.44 = (f32[512,1024]{1,0:T(8,128)S(1)}, f32[512,1024]{1,0:T(8,128)}, u32[]{:S(2)}) copy-start(f32[512,1024]{1,0:T(8,128)} %fusion.36) | copy-start | bytes 6291460
  700.1 47.2 %collective-permute-start.5 = (bf16[1024,512]{1,0:T(8,128)(2,1)S(1)}, bf16[1024,512]{1,0:T(8,128)(2,1)S(1)}, u32[]{:S(2)}, u32[]{:S(2)}) collective-permute-start(bf16[1024,512]{1,0:T(8,128)(2,1)S(1)} %pad_maximum_fusion.1), channel_id=1, source_target_pairs={{0,16},{4,20},{8,24},{12,28},{16,0},{20,4},{24,8},{28,12},{1,17},{... | collective-permute-start | bytes 3145736 | tf_op jit(solution)/shard_map/ppermute | solution.py:16
  754.0 50.4 %all-gather.37.cloned.1.call-start = ((), (), s32[]{:S(2)}) async-start(), calls=%async_computation.30 | async-start | bytes 1310720 | tf_op jit(solution)/shard_map/all_gather | solution.py:114
  787.6 56.5 %reduce-scatter.51.cloned.1.call-start = ((), (), s32[]{:S(2)}) async-start(), calls=%async_computation.31 | async-start | bytes 1310720 | tf_op jit(solution)/shard_map/reduce_scatter | solution.py:127
  806.4 4.3 copy-start.3
  806.4 4.3 copy-start.32
  814.6 4.5 copy-start.26
  815.6 3.6 copy-start.28
  819.2 77.2 %all-gather.53.cloned.1.call-start = ((), (), s32[]{:S(2)}) async-start(), calls=%async_computation.43 | async-start | bytes 2359296 | tf_op jit(solution)/shard_map/all_gather | solution.py:226
  819.8 93.7 %all-gather.39.cloned.1.call-start = ((), (), s32[]{:S(2)}) async-start(), calls=%async_computation.32 | async-start | bytes 1310720 | tf_op jit(solution)/shard_map/all_gather | solution.py:114
  847.3 99.5 %reduce-scatter.53.cloned.1.call-start = ((), (), s32[]{:S(2)}) async-start(), calls=%async_computation.33 | async-start | bytes 1310720 | tf_op jit(solution)/shard_map/reduce_scatter | solution.py:127
  913.4 6.1 copy-start.37
  921.9 45.0 %copy-start.8 = (bf16[1,256,1024]{2,1,0:T(8,128)(2,1)S(1)}, bf16[1,256,1024]{2,1,0:T(8,128)(2,1)}, u32[]{:S(2)}) copy-start(bf16[1,256,1024]{2,1,0:T(8,128)(2,1)} %copy-done.7) | copy-start | bytes 1572868
  921.9 45.0 %copy-start.14 = (bf16[4,64,512]{2,1,0:T(8,128)(2,1)S(1)}, bf16[4,64,512]{2,1,0:T(8,128)(2,1)}, u32[]{:S(2)}) copy-start(bf16[4,64,512]{2,1,0:T(8,128)(2,1)} %copy-done.13) | copy-start | bytes 786436
  921.9 45.0 %all-gather.41.cloned.1.call-start = ((), (), s32[]{:S(2)}) async-start(), calls=%async_computation.34 | async-start | bytes 1310720 | tf_op jit(solution)/shard_map/all_gather | solution.py:114
  950.0 64.5 %reduce-scatter.55.cloned.1.call-start = ((), (), s32[]{:S(2)}) async-start(), calls=%async_computation.35 | async-start | bytes 1310720 | tf_op jit(solution)/shard_map/reduce_scatter | solution.py:127
  968.6 3.6 copy-start.1
  968.6 3.6 copy-start.30
  975.5 3.5 copy-start.24
  979.0 97.6 %reduce-scatter.75.cloned.1.call-start = ((), (), s32[]{:S(2)}) async-start(), calls=%async_computation.51 | async-start | bytes 2359296
  985.2 2.9 copy-start.27
  985.2 156.2 %reduce-scatter.67.cloned.1.call-start = ((), (), s32[]{:S(2)}) async-start(), calls=%async_computation.47 | async-start | bytes 73728
  986.2 220.9 %reduce-scatter.71.cloned.1.call-start = ((), (), s32[]{:S(2)}) async-start(), calls=%async_computation.49 | async-start | bytes 589824
  988.0 286.9 %reduce-scatter.63.cloned.1.call-start = ((), (), s32[]{:S(2)}) async-start(), calls=%async_computation.45 | async-start | bytes 1769472
  996.1 343.9 %reduce-scatter.65.cloned.1.call-start = ((), (), s32[]{:S(2)}) async-start(), calls=%async_computation.46 | async-start | bytes 73728
  997.1 413.7 %reduce-scatter.73.cloned.1.call-start = ((), (), s32[]{:S(2)}) async-start(), calls=%async_computation.50 | async-start | bytes 2359296
  1003.3 478.4 %reduce-scatter.59.cloned.1.call-start = ((), (), s32[]{:S(2)}) async-start(), calls=%async_computation.37 | async-start | bytes 2359296 | tf_op jit(solution)/shard_map/reduce_scatter | solution.py:288
  1007.5 544.9 %reduce-scatter.57.cloned.1.call-start = ((), (), s32[]{:S(2)}) async-start(), calls=%async_computation.36 | async-start | bytes 2359296 | tf_op jit(solution)/shard_map/reduce_scatter | solution.py:288
  1011.7 606.4 %reduce-scatter.69.cloned.1.call-start = ((), (), s32[]{:S(2)}) async-start(), calls=%async_computation.48 | async-start | bytes 589824
  1014.4 740.6 %reduce-scatter.77.cloned.1.call-start = ((), (), s32[]{:S(2)}) async-start(), calls=%async_computation.52 | async-start | bytes 540672
  1017.8 2.2 copy-start.25
  1017.8 871.1 %reduce-scatter.79.cloned.1.call-start = ((), (), s32[]{:S(2)}) async-start(), calls=%async_computation.53 | async-start | bytes 540672
  1019.9 934.0 %reduce-scatter.61.cloned.1.call-start = ((), (), s32[]{:S(2)}) async-start(), calls=%async_computation.44 | async-start | bytes 1769472
  1410.9 208.9 %copy-start.12 = (bf16[128,1024]{1,0:T(8,128)(2,1)S(1)}, bf16[128,1024]{1,0:T(8,128)(2,1)}, u32[]{:S(2)}) copy-start(bf16[128,1024]{1,0:T(8,128)(2,1)} %reduce-scatter.55.cloned.1.call-done) | copy-start | bytes 786436
  (25 other events, 35.5 us)
Sparse Core Ops, SparseCore 0:
  149.3 14.1 all-gather.26
  166.1 45.3 all-gather.42
  257.1 30.7 reduce-scatter.40
  290.4 81.8 all-gather.44
  374.3 20.4 all-gather.28
  406.4 31.1 reduce-scatter.42
  440.3 46.9 all-gather.46
  489.4 14.8 all-gather.30
  513.3 31.1 reduce-scatter.44
  547.0 53.0 all-gather.48
  602.2 16.8 all-gather.32
  620.5 16.6 all-gather.34
  639.9 50.3 all-gather.50
  698.8 22.9 reduce-scatter.48
  754.2 30.4 reduce-scatter.46
  787.7 16.6 all-gather.36
  819.3 24.7 reduce-scatter.50
  846.0 50.3 all-gather.52
  898.5 14.8 all-gather.38
  922.0 24.7 reduce-scatter.52
  950.1 16.6 all-gather.40
  979.1 24.8 reduce-scatter.54
  1007.5 69.0 reduce-scatter.74
  1079.9 61.4 reduce-scatter.66
  1145.3 61.6 reduce-scatter.70
  1210.3 64.5 reduce-scatter.62
  1278.7 61.2 reduce-scatter.64
  1343.5 67.3 reduce-scatter.72
  1414.4 67.2 reduce-scatter.58
  1485.1 67.2 reduce-scatter.56
  1556.3 61.7 reduce-scatter.68
  1620.3 134.6 reduce-scatter.76
  1757.1 131.6 reduce-scatter.78
  1892.3 61.5 reduce-scatter.60
